TPU v7x, 32 devices: a whole 2x2x4 slice. The times are simulated.
32 devices in a mesh: seq: 8 (over z, y), head: 4 (over x, core).
Axes of the slice: x: 2, y: 2, z: 4, core: 2. Of those that a mesh axis runs over, the one named last changes fastest.
Arguments:
- queries: bfloat16 [4096, 4096], P('seq', 'head'), may hold values from -6 to 6
- keys: bfloat16 [4096, 4096], P('seq', 'head'), may hold values from -6 to 6
- values: bfloat16 [4096, 4096], P('seq', 'head'), may hold values from -6 to 6
- level_weights: float32 [5, 32, 4096], P(None, 'head', 'seq'), may hold values from 0.1 to 3, as said below
- norm_gain: float32 [4096], P('head'), may hold values from 0.25 to 1.75
Outputs:
- mixed: bfloat16 [4096, 4096], P('seq', 'head')
Inputs may be any that keep to these rules, and one draw needn't show every extreme that they name: `level_weights`: positive level weights.
All inputs are finite; a program needn't handle non-finite values.
Results may differ from a plain program's by a relative error of at most 0.0049.
Values may be sent and summed in bfloat16 or wider, within the bound.
No kernel may reach another device: no remote copies, remote signals or barrier semaphores. Data moves between devices by JAX's collectives and lax.ppermute only.
A program may use at most 64 MiB of HBM per device.

v0:
```python
import jax
import jax.numpy as jnp
from jax import lax
from jax.sharding import PartitionSpec as P

HEAD_DIM = 128
STRETCH = 256
D = 4096
EPSILON = 1e-06


def swapped(block, axis, stride):
    count = lax.axis_size(axis)
    route = []
    for low in range(count):
        high = low | 1 << stride
        if high != low and high < count:
            route += [(low, high), (high, low)]
    return lax.ppermute(block, axis, route)


def shifted(block, axis, distance):
    devices = range(lax.axis_size(axis))
    route = [(i - distance, i) for i in devices if i - distance in devices]
    return lax.ppermute(block, axis, route)


def local(queries, keys, values, level_weights, norm_gain):
    tok_rows = queries.shape[0]
    heads_here = queries.shape[1] // HEAD_DIM
    stretch_count = tok_rows // STRETCH
    block_shape = (stretch_count, STRETCH, heads_here, HEAD_DIM)
    query_block_list = queries.reshape(block_shape)
    key_blocks = keys.reshape(block_shape)
    value_blocks = values.reshape(block_shape)
    level_total = level_weights.shape[0]
    weights_here = level_weights.reshape(level_total, heads_here, stretch_count, STRETCH).transpose(
        0, 2, 3, 1
    )
    states = jnp.einsum(
        "cthk,cthv->chkv", key_blocks, value_blocks, preferred_element_type=jnp.float32
    )
    scores = jnp.einsum(
        "cthk,cshk->chts", query_block_list, key_blocks, preferred_element_type=jnp.float32
    )
    causal = lax.broadcasted_iota(jnp.int32, (STRETCH, STRETCH), 0) >= lax.broadcasted_iota(
        jnp.int32, (STRETCH, STRETCH), 1
    )
    attn_probs = jnp.where(causal[None, None], scores, 0.0).astype(jnp.bfloat16)
    intra_out = jnp.einsum(
        "chts,cshv->cthv", attn_probs, value_blocks, preferred_element_type=jnp.float32
    )
    combined = weights_here[0][..., None] * intra_out
    running = states
    local_bits = stretch_count.bit_length() - 1
    level_bit = 0
    groups = running.shape[0] // 2
    block_span = 2**level_bit
    halves = running.reshape(groups, 2, heads_here, HEAD_DIM, HEAD_DIM)
    leftward_sum = halves[:, 0].astype(jnp.bfloat16)
    rightward_queries = query_block_list.reshape(
        groups, 2, block_span * STRETCH, heads_here, HEAD_DIM
    )[:, 1]
    state_readout = jnp.einsum(
        "nthk,nhkv->nthv", rightward_queries, leftward_sum, preferred_element_type=jnp.float32
    )
    level_weight = weights_here[1 + level_bit].reshape(groups, 2, block_span * STRETCH, heads_here)[
        :, 1
    ]
    contrib = level_weight[..., None] * state_readout
    padded = jnp.stack([jnp.zeros_like(contrib), contrib], axis=1)
    combined = combined + padded.reshape(stretch_count, STRETCH, heads_here, HEAD_DIM)
    running = halves[:, 0] + halves[:, 1]
    device_sum = running[0]
    seq_count = lax.axis_size("seq")
    seq_bits = seq_count.bit_length() - 1
    position = lax.axis_index("seq")
    crossing_state_list = []
    for level_bit in range(seq_bits - 1):
        partner = swapped(device_sum, "seq", level_bit)
        is_right = position >> level_bit & 1 == 1
        crossing_state_list.append(
            jnp.where(is_right, partner, jnp.zeros_like(partner)).astype(jnp.bfloat16)
        )
        device_sum = device_sum + partner
    last_partner = shifted(device_sum.astype(jnp.bfloat16), "seq", seq_count // 2)
    crossing_state_list.append(last_partner)
    for number, state_per_level in enumerate(crossing_state_list):
        state_readout = jnp.einsum(
            "lwnx,nxq->lwnq", query_block_list, state_per_level, preferred_element_type=jnp.float32
        )
        combined = combined + weights_here[1 + local_bits + number][..., None] * state_readout
    squares = jnp.sum(combined * combined, axis=(2, 3)).reshape(tok_rows)
    total_squares = lax.psum(squares, "head")
    inverse_rms = lax.rsqrt(total_squares / D + EPSILON)
    flat_out = combined.reshape(tok_rows, heads_here * HEAD_DIM)
    mixed_out = flat_out * inverse_rms[:, None] * norm_gain[None, :]
    return mixed_out.astype(jnp.bfloat16)


def solution(mesh):
    return jax.shard_map(
        local,
        mesh=mesh,
        in_specs=(
            P("seq", "head"),
            P("seq", "head"),
            P("seq", "head"),
            P(None, "head", "seq"),
            P("head"),
        ),
        out_specs=P("seq", "head"),
        check_vma=False,
    )
```

profile of v0, /device:TPU:24, one launch (start us, length us, event | category | flops | bytes accessed | tf_op | source)
XLA Modules:
  0.0 59.7 jit_solution(3533077832521115567)
XLA Ops:
  0.0 1.6 %copy.53 = bf16[64,8,8,128]{3,2,1,0:T(8,128)(2,1)S(1)} copy(bf16[64,8,8,128]{3,1,2,0:T(8,128)(2,1)} %bitcast.103) | data formatting | bytes 2097152
  1.6 0.7 %copy.20 = bf16[2,256,8,128]{1,3,2,0:T(8,128)(2,1)S(1)} copy(bf16[2,256,8,128]{3,2,1,0:T(8,128)(2,1)S(1)} %bitcast.102) | data formatting | bytes 2097152 | tf_op jit(solution)/shard_map/reshape | solution.py:34
  2.3 0.0 copy-start
  2.3 0.3 copy.54
  2.6 0.4 convolution_bitcast_fusion.1
  3.0 0.2 copy-done
  3.2 0.8 %fusion.17 = f32[8,128,128]{2,1,0:T(8,128)} fusion(f32[1,2,8,128,128]{4,3,2,1,0:T(8,128)S(1)} %convolution_bitcast_fusion.1), kind=kLoop, calls=%fused_computation.27 | loop fusion | flops 131072 | bytes 1572864 | tf_op jit(solution)/shard_map/add | solution.py:73
  4.1 1.5 %collective-permute-start = (f32[8,128,128]{2,1,0:T(8,128)}, f32[8,128,128]{2,1,0:T(8,128)}, u32[]{:S(2)}, u32[]{:S(2)}) collective-permute-start(f32[8,128,128]{2,1,0:T(8,128)} %fusion.17), channel_id=1, source_target_pairs={{0,4},{4,0},{8,12},{12,8},{16,20},{20,16},{24,28},{28,24},{1,5},{5... | collective-permute-start | bytes 1572872 | tf_op jit(solution)/shard_map/ppermute | solution.py:19
  5.7 0.3 copy.52
  6.0 0.3 fusion.7
  6.4 4.2 %fusion.5 = f32[2,8,256,128]{2,3,1,0:T(8,128)} fusion(bf16[2,256,8,128]{1,3,2,0:T(8,128)(2,1)} %copy-done, pred[256,256]{1,0:T(8,128)(4,1)S(1)} %iota_compare_fusion, bf16[2,256,8,128]{3,2,1,0:T(8,128)(2,1)} %bitcast.101, bf16[2,256,8,128]{3,2,1,0:T(8,128)(2,1)S(1)} %bitcast.95), kind=kOutput, calls=%fused_computation.13 | convolution fusion | flops 538968064 | bytes 5308416 | tf_op jit(solution)/shard_map/chts,cshv->cthv/dot_general | solution.py:50
  10.6 7.5 %collective-permute-done = f32[8,128,128]{2,1,0:T(8,128)} collective-permute-done((f32[8,128,128]{2,1,0:T(8,128)}, f32[8,128,128]{2,1,0:T(8,128)}, u32[]{:S(2)}, u32[]{:S(2)}) %collective-permute-start) | collective-permute-done | bytes 524320 | tf_op jit(solution)/shard_map/ppermute | solution.py:19
  18.1 1.1 %fusion.34 = f32[8,128,128]{2,1,0:T(8,128)S(1)} fusion(f32[8,128,128]{2,1,0:T(8,128)} %collective-permute-done, f32[1,2,8,128,128]{4,3,2,1,0:T(8,128)S(1)} %convolution_bitcast_fusion.1), kind=kLoop, calls=%fused_computation.51 | loop fusion | flops 262144 | bytes 2097152 | tf_op jit(solution)/shard_map/add | solution.py:85
  19.2 0.5 collective-permute-start.1
  19.7 0.5 fusion.13
  20.2 11.8 %collective-permute-done.1 = f32[8,128,128]{2,1,0:T(8,128)S(1)} collective-permute-done((f32[8,128,128]{2,1,0:T(8,128)S(1)}, f32[8,128,128]{2,1,0:T(8,128)S(1)}, u32[]{:S(2)}, u32[]{:S(2)}) %collective-permute-start.1) | collective-permute-done | bytes 524320 | tf_op jit(solution)/shard_map/ppermute | solution.py:19
  32.1 0.1 add_convert_fusion
  32.1 1.4 %collective-permute-start.2 = (bf16[8,128,128]{2,1,0:T(8,128)(2,1)S(1)}, bf16[8,128,128]{2,1,0:T(8,128)(2,1)S(1)}, u32[]{:S(2)}, u32[]{:S(2)}) collective-permute-start(bf16[8,128,128]{2,1,0:T(8,128)(2,1)S(1)} %add_convert_fusion), channel_id=1, source_target_pairs={{0,16},{4,20},{8,24},{12,28},{1,17},{5,21},{9,25},{13,29},{2,18},{... | collective-permute-start | bytes 786440 | tf_op jit(solution)/shard_map/ppermute | solution.py:25
  33.6 0.5 fusion.11
  34.1 12.8 %collective-permute-done.2 = bf16[8,128,128]{2,1,0:T(8,128)(2,1)S(1)} collective-permute-done((bf16[8,128,128]{2,1,0:T(8,128)(2,1)S(1)}, bf16[8,128,128]{2,1,0:T(8,128)(2,1)S(1)}, u32[]{:S(2)}, u32[]{:S(2)}) %collective-permute-start.2) | collective-permute-done | bytes 262176 | tf_op jit(solution)/shard_map/ppermute | solution.py:25
  46.9 2.4 %multiply_reduce_fusion = (f32[2,256]{1,0:T(2,128)S(1)}, f32[2,256,8,128]{1,3,2,0:T(8,128)}) fusion(bf16[2,256,8,128]{3,2,1,0:T(8,128)(2,1)S(1)} %bitcast.98, bf16[8,128,128]{2,1,0:T(8,128)(2,1)S(1)} %collective-permute-done.2, f32[2,256,8]{1,2,0:T(8,128)S(1)} %get-tuple-element.6, f32[8,128,2,256]{3,1,0,2:T(8,128)S(1)} %fusion.11, ...), kind=kOutput, calls=%fused_computation.12 | convolution fusion | flops 139460096 | bytes 10815488 | tf_op jit(solution)/shard_map/lwnx,nxq->lwnq/dot_general | solution.py:89
  49.3 6.8 %psum.7 = f32[512]{0:T(512)S(1)} all-reduce(f32[512]{0:T(512)S(1)} %bitcast.109), channel_id=1, replica_groups=mesh['seq'=8,'head'=4] {'head'}, use_global_device_ids=true, to_apply=%region_1.2 | all-reduce | flops 512 | bytes 4096 | tf_op jit(solution)/shard_map/psum | solution.py:94
  56.1 2.1 %copy.33 = f32[2,256,8,128]{3,2,1,0:T(8,128)S(1)} copy(f32[2,256,8,128]{1,3,2,0:T(8,128)} %get-tuple-element.10) | data formatting | bytes 4194304 | tf_op jit(solution)/shard_map/add | solution.py:92
  58.3 1.4 %fusion.1 = bf16[512,1024]{1,0:T(8,128)(2,1)} fusion(f32[64,8,8,128]{3,2,1,0:T(8,128)S(1)} %bitcast.99, f32[1024]{0:T(1024)S(1)} %copy-done.6, f32[512]{0:T(512)S(1)} %add_rsqrt_fusion), kind=kLoop, calls=%fused_computation.3 | loop fusion | flops 1572864 | bytes 3151872 | tf_op jit(solution)/shard_map/convert_element_type | solution.py:98
  (18 shorter events, 0.1 us)
Async XLA Ops:
  0.0 2.3 %copy-start.3 = (bf16[512,1024]{1,0:T(8,128)(2,1)S(1)}, bf16[512,1024]{1,0:T(8,128)(2,1)}, u32[]{:S(2)}) copy-start(bf16[512,1024]{1,0:T(8,128)(2,1)} %param.7) | copy-start | bytes 3145732
  2.3 1.0 %copy-start = (bf16[2,256,8,128]{1,3,2,0:T(8,128)(2,1)}, bf16[2,256,8,128]{1,3,2,0:T(8,128)(2,1)S(1)}, u32[]{:S(2)}) copy-start(bf16[2,256,8,128]{1,3,2,0:T(8,128)(2,1)S(1)} %copy.20) | copy-start | bytes 3145732
  2.6 1.5 %copy-start.1 = (bf16[64,8,8,128]{3,2,1,0:T(8,128)(2,1)}, bf16[64,8,8,128]{3,2,1,0:T(8,128)(2,1)S(1)}, u32[]{:S(2)}) copy-start(bf16[64,8,8,128]{3,2,1,0:T(8,128)(2,1)S(1)} %copy.54) | copy-start | bytes 3145732
  2.6 3.1 %copy-start.5 = (f32[5,8,512]{2,1,0:T(8,128)S(1)}, f32[5,8,512]{2,1,0:T(8,128)}, u32[]{:S(2)}) copy-start(f32[5,8,512]{2,1,0:T(8,128)} %param.8) | copy-start | bytes 245764
  2.6 3.1 %copy-start.4 = (bf16[512,1024]{1,0:T(8,128)(2,1)S(1)}, bf16[512,1024]{1,0:T(8,128)(2,1)}, u32[]{:S(2)}) copy-start(bf16[512,1024]{1,0:T(8,128)(2,1)} %param.5) | copy-start | bytes 3145732
  4.1 14.0 %collective-permute-start = (f32[8,128,128]{2,1,0:T(8,128)}, f32[8,128,128]{2,1,0:T(8,128)}, u32[]{:S(2)}, u32[]{:S(2)}) collective-permute-start(f32[8,128,128]{2,1,0:T(8,128)} %fusion.17), channel_id=1, source_target_pairs={{0,4},{4,0},{8,12},{12,8},{16,20},{20,16},{24,28},{28,24},{1,5},{5... | collective-permute-start | bytes 1572872 | tf_op jit(solution)/shard_map/ppermute | solution.py:19
  19.2 12.9 %collective-permute-start.1 = (f32[8,128,128]{2,1,0:T(8,128)S(1)}, f32[8,128,128]{2,1,0:T(8,128)S(1)}, u32[]{:S(2)}, u32[]{:S(2)}) collective-permute-start(f32[8,128,128]{2,1,0:T(8,128)S(1)} %fusion.34), channel_id=1, source_target_pairs={{0,8},{8,0},{4,12},{12,4},{16,24},{24,16},{20,28},{28,20},{1,9},{9... | collective-permute-start | bytes 1572872 | tf_op jit(solution)/shard_map/ppermute | solution.py:19
  32.1 14.8 %copy-start.2 = (f32[2,8,256,128]{2,3,1,0:T(8,128)S(1)}, f32[2,8,256,128]{2,3,1,0:T(8,128)}, u32[]{:S(2)}) copy-start(f32[2,8,256,128]{2,3,1,0:T(8,128)} %fusion.5) | copy-start | bytes 6291460
  32.1 14.8 %collective-permute-start.2 = (bf16[8,128,128]{2,1,0:T(8,128)(2,1)S(1)}, bf16[8,128,128]{2,1,0:T(8,128)(2,1)S(1)}, u32[]{:S(2)}, u32[]{:S(2)}) collective-permute-start(bf16[8,128,128]{2,1,0:T(8,128)(2,1)S(1)} %add_convert_fusion), channel_id=1, source_target_pairs={{0,16},{4,20},{8,24},{12,28},{1,17},{5,21},{9,25},{13,29},{2,18},{... | collective-permute-start | bytes 786440 | tf_op jit(solution)/shard_map/ppermute | solution.py:25
  56.1 2.1 %copy-start.6 = (f32[1024]{0:T(1024)S(1)}, f32[1024]{0:T(1024)}, u32[]{:S(2)}) copy-start(f32[1024]{0:T(1024)} %param.9) | copy-start | bytes 12292
where the time goes:
time: 60 us; the launch traced here: 59.7 us
  waiting for transfers between devices  32.2 us (54%)
  matrix products  8.38 us (14%)
  blocking collectives  6.83 us (11%)
  local copies, waits for them, and re-layouts  5.2 us (9%)
  starting transfers between devices  3.46 us (6%)
  other arithmetic  3.45 us (6%)
    ppermute x2, waiting for transfers between devices, swapped(): return lax.ppermute(block, axis, route)  19.3 us
    ppermute x1, waiting for transfers between devices, shifted(): return lax.ppermute(block, axis, route)  12.8 us
    psum x1, blocking collectives, local(): total_squares = lax.psum(squares, 'head')  6.83 us
    dot_general x1, matrix products, local(): jnp.einsum('chts,cshv->cthv', attn_probs, value_blocks, preferred_element...  4.22 us
    dot_general x3, matrix products, local(): jnp.einsum('lwnx,nxq->lwnq', query_block_list, state_per_level, preferred...  3.39 us
    unnamed x18, local copies, waits for them, and re-layouts  2.36 us
    add x1, local copies, waits for them, and re-layouts, local(): combined + weights_here[1 + local_bits + number][..., None] * state_readout  2.12 us
    ppermute x2, starting transfers between devices, swapped(): return lax.ppermute(block, axis, route)  2.03 us
  transfers between devices with their start and end apart: 3, of which 3 were waited for; matrix products, arithmetic and copies ran while one was open for 10% of the time, Pallas kernels for 0%

commit v1 on v0

--- a/solution.py
+++ b/solution.py
@@ -91,7 +91,18 @@
         )
         combined = combined + weights_here[1 + local_bits + number][..., None] * state_readout
     squares = jnp.sum(combined * combined, axis=(2, 3)).reshape(tok_rows)
-    total_squares = lax.psum(squares, "head")
+
+    def _press_stacks_all(local_block):
+        ndev = lax.axis_size("head")
+        oldest, piece_now = (local_block, 0)
+        while 1 << piece_now < ndev:
+            current_arr = tuple(((w, w ^ 1 << piece_now) for w in range(ndev)))
+            finding = lax.ppermute(oldest, "head", current_arr)
+            oldest = oldest + finding
+            piece_now = piece_now + 1
+        return oldest
+
+    total_squares = _press_stacks_all(squares)
     inverse_rms = lax.rsqrt(total_squares / D + EPSILON)
     flat_out = combined.reshape(tok_rows, heads_here * HEAD_DIM)
     mixed_out = flat_out * inverse_rms[:, None] * norm_gain[None, :]

time: 60 us -> 55.9 us (0.932)
  blocking collectives: 6.83 us -> 0 us
  starting transfers between devices: 3.46 us -> 4.97 us
  waiting for transfers between devices: 32.2 us -> 33.3 us
    psum x1 -> x0, blocking collectives: 6.83 us -> none  [local(): total_squares = lax.psum(squares, 'head')]
    ppermute x0 -> x2, starting transfers between devices: none -> 1.51 us  [_press_stacks_all(): finding = lax.ppermute(oldest, 'head', current_arr)]
    ppermute x0 -> x2, waiting for transfers between devices: none -> 1.15 us  [_press_stacks_all(): finding = lax.ppermute(oldest, 'head', current_arr)]
  transfers between devices with their start and end apart: 3 -> 5, of which waited for: 3 -> 4; matrix products, arithmetic and copies ran while one was open for 10% -> 14% of each run, Pallas kernels for 0% -> 0%
where the time goes in v1:
time: 55.9 us; the launch traced here: 55.5 us
  waiting for transfers between devices  33.3 us (60%)
  matrix products  8.32 us (15%)
  local copies, waits for them, and re-layouts  5.2 us (9%)
  starting transfers between devices  4.97 us (9%)
  other arithmetic  3.48 us (6%)
    ppermute x2, waiting for transfers between devices, swapped(): return lax.ppermute(block, axis, route)  19.4 us
    ppermute x1, waiting for transfers between devices, shifted(): return lax.ppermute(block, axis, route)  12.8 us
    dot_general x1, matrix products, local(): jnp.einsum('chts,cshv->cthv', attn_probs, value_blocks, preferred_element...  4.19 us
    dot_general x3, matrix products, local(): jnp.einsum('lwnx,nxq->lwnq', query_block_list, state_per_level, preferred...  3.36 us
    unnamed x18, local copies, waits for them, and re-layouts  2.36 us
    add x1, local copies, waits for them, and re-layouts, local(): combined + weights_here[1 + local_bits + number][..., None] * state_readout  2.12 us
    ppermute x2, starting transfers between devices, swapped(): return lax.ppermute(block, axis, route)  2.03 us
    ppermute x2, starting transfers between devices, _press_stacks_all(): finding = lax.ppermute(oldest, 'head', current_arr)  1.51 us
  transfers between devices with their start and end apart: 5, of which 4 were waited for; matrix products, arithmetic and copies ran while one was open for 14% of the time, Pallas kernels for 0%

profile of v1, /device:TPU:24, one launch (start us, length us, event | category | flops | bytes accessed | tf_op | source)
XLA Modules:
  0.0 55.5 jit_solution(5017500552953542509)
XLA Ops:
  0.0 1.6 %copy.53 = bf16[64,8,8,128]{3,2,1,0:T(8,128)(2,1)S(1)} copy(bf16[64,8,8,128]{3,1,2,0:T(8,128)(2,1)} %bitcast.103) | data formatting | bytes 2097152
  1.6 0.7 %copy.20 = bf16[2,256,8,128]{1,3,2,0:T(8,128)(2,1)S(1)} copy(bf16[2,256,8,128]{3,2,1,0:T(8,128)(2,1)S(1)} %bitcast.102) | data formatting | bytes 2097152 | tf_op jit(solution)/shard_map/reshape | solution.py:34
  2.3 0.3 copy.54
  2.6 0.4 convolution_bitcast_fusion.1
  3.0 0.2 copy-done
  3.2 0.9 %fusion.17 = f32[8,128,128]{2,1,0:T(8,128)} fusion(f32[1,2,8,128,128]{4,3,2,1,0:T(8,128)S(1)} %convolution_bitcast_fusion.1), kind=kLoop, calls=%fused_computation.27 | loop fusion | flops 131072 | bytes 1572864 | tf_op jit(solution)/shard_map/add | solution.py:73
  4.1 1.5 %collective-permute-start = (f32[8,128,128]{2,1,0:T(8,128)}, f32[8,128,128]{2,1,0:T(8,128)}, u32[]{:S(2)}, u32[]{:S(2)}) collective-permute-start(f32[8,128,128]{2,1,0:T(8,128)} %fusion.17), channel_id=1, source_target_pairs={{0,4},{4,0},{8,12},{12,8},{16,20},{20,16},{24,28},{28,24},{1,5},{5... | collective-permute-start | bytes 1572872 | tf_op jit(solution)/shard_map/ppermute | solution.py:19
  5.7 0.3 copy.52
  6.0 0.3 fusion.7
  6.4 4.2 %fusion.5 = f32[2,8,256,128]{2,3,1,0:T(8,128)} fusion(bf16[2,256,8,128]{1,3,2,0:T(8,128)(2,1)} %copy-done, pred[256,256]{1,0:T(8,128)(4,1)S(1)} %iota_compare_fusion, bf16[2,256,8,128]{3,2,1,0:T(8,128)(2,1)} %bitcast.101, bf16[2,256,8,128]{3,2,1,0:T(8,128)(2,1)S(1)} %bitcast.95), kind=kOutput, calls=%fused_computation.13 | convolution fusion | flops 538968064 | bytes 5308416 | tf_op jit(solution)/shard_map/chts,cshv->cthv/dot_general | solution.py:50
  10.6 7.5 %collective-permute-done = f32[8,128,128]{2,1,0:T(8,128)} collective-permute-done((f32[8,128,128]{2,1,0:T(8,128)}, f32[8,128,128]{2,1,0:T(8,128)}, u32[]{:S(2)}, u32[]{:S(2)}) %collective-permute-start) | collective-permute-done | bytes 524320 | tf_op jit(solution)/shard_map/ppermute | solution.py:19
  18.1 1.1 %fusion.34 = f32[8,128,128]{2,1,0:T(8,128)S(1)} fusion(f32[8,128,128]{2,1,0:T(8,128)} %collective-permute-done, f32[1,2,8,128,128]{4,3,2,1,0:T(8,128)S(1)} %convolution_bitcast_fusion.1), kind=kLoop, calls=%fused_computation.51 | loop fusion | flops 262144 | bytes 2097152 | tf_op jit(solution)/shard_map/add | solution.py:85
  19.2 0.5 collective-permute-start.1
  19.7 0.5 fusion.13
  20.3 11.8 %collective-permute-done.1 = f32[8,128,128]{2,1,0:T(8,128)S(1)} collective-permute-done((f32[8,128,128]{2,1,0:T(8,128)S(1)}, f32[8,128,128]{2,1,0:T(8,128)S(1)}, u32[]{:S(2)}, u32[]{:S(2)}) %collective-permute-start.1) | collective-permute-done | bytes 524320 | tf_op jit(solution)/shard_map/ppermute | solution.py:19
  32.1 0.1 add_convert_fusion
  32.2 1.4 %collective-permute-start.2 = (bf16[8,128,128]{2,1,0:T(8,128)(2,1)S(1)}, bf16[8,128,128]{2,1,0:T(8,128)(2,1)S(1)}, u32[]{:S(2)}, u32[]{:S(2)}) collective-permute-start(bf16[8,128,128]{2,1,0:T(8,128)(2,1)S(1)} %add_convert_fusion), channel_id=1, source_target_pairs={{0,16},{4,20},{8,24},{12,28},{1,17},{5,21},{9,25},{13,29},{2,18},{... | collective-permute-start | bytes 786440 | tf_op jit(solution)/shard_map/ppermute | solution.py:25
  33.6 0.5 fusion.11
  34.1 12.8 %collective-permute-done.2 = bf16[8,128,128]{2,1,0:T(8,128)(2,1)S(1)} collective-permute-done((bf16[8,128,128]{2,1,0:T(8,128)(2,1)S(1)}, bf16[8,128,128]{2,1,0:T(8,128)(2,1)S(1)}, u32[]{:S(2)}, u32[]{:S(2)}) %collective-permute-start.2) | collective-permute-done | bytes 262176 | tf_op jit(solution)/shard_map/ppermute | solution.py:25
  46.9 2.4 %multiply_reduce_fusion = (f32[2,256]{1,0:T(2,128)S(1)}, f32[2,256,8,128]{1,3,2,0:T(8,128)}) fusion(bf16[2,256,8,128]{3,2,1,0:T(8,128)(2,1)S(1)} %bitcast.98, bf16[8,128,128]{2,1,0:T(8,128)(2,1)S(1)} %collective-permute-done.2, f32[2,256,8]{1,2,0:T(8,128)S(1)} %get-tuple-element.6, f32[8,128,2,256]{3,1,0,2:T(8,128)S(1)} %fusion.11, ...), kind=kOutput, calls=%fused_computation.12 | convolution fusion | flops 139460096 | bytes 10815488 | tf_op jit(solution)/shard_map/lwnx,nxq->lwnq/dot_general | solution.py:89
  49.3 1.1 %collective-permute-done.3 = f32[512]{0:T(512)S(1)} collective-permute-done((f32[512]{0:T(512)S(1)}, f32[512]{0:T(512)S(1)}, u32[]{:S(2)}, u32[]{:S(2)}) %collective-permute-start.3) | collective-permute-done | bytes 2080 | tf_op jit(solution)/shard_map/ppermute | solution.py:100
  50.5 1.5 %collective-permute-start.4 = (f32[512]{0:T(512)S(1)}, f32[512]{0:T(512)S(1)}, u32[]{:S(2)}, u32[]{:S(2)}) collective-permute-start(f32[512]{0:T(512)S(1)} %add.49), channel_id=1, source_target_pairs={{0,2},{1,3},{2,0},{3,1},{4,6},{5,7},{6,4},{7,5},{8,10},{9,11},{10,... | collective-permute-start | bytes 6152 | tf_op jit(solution)/shard_map/ppermute | solution.py:100
  52.0 2.1 %copy.33 = f32[2,256,8,128]{3,2,1,0:T(8,128)S(1)} copy(f32[2,256,8,128]{1,3,2,0:T(8,128)} %get-tuple-element.10) | data formatting | bytes 4194304 | tf_op jit(solution)/shard_map/add | solution.py:92
  54.1 1.4 %fusion.1 = bf16[512,1024]{1,0:T(8,128)(2,1)} fusion(f32[64,8,8,128]{3,2,1,0:T(8,128)S(1)} %bitcast.99, f32[1024]{0:T(1024)S(1)} %copy-done.6, f32[512]{0:T(512)S(1)} %add_rsqrt_fusion), kind=kLoop, calls=%fused_computation.3 | loop fusion | flops 1572864 | bytes 3151872 | tf_op jit(solution)/shard_map/convert_element_type | solution.py:109
  (22 shorter events, 0.1 us)
Async XLA Ops:
  0.0 2.3 %copy-start.3 = (bf16[512,1024]{1,0:T(8,128)(2,1)S(1)}, bf16[512,1024]{1,0:T(8,128)(2,1)}, u32[]{:S(2)}) copy-start(bf16[512,1024]{1,0:T(8,128)(2,1)} %param.7) | copy-start | bytes 3145732
  2.3 1.0 %copy-start = (bf16[2,256,8,128]{1,3,2,0:T(8,128)(2,1)}, bf16[2,256,8,128]{1,3,2,0:T(8,128)(2,1)S(1)}, u32[]{:S(2)}) copy-start(bf16[2,256,8,128]{1,3,2,0:T(8,128)(2,1)S(1)} %copy.20) | copy-start | bytes 3145732
  2.6 1.6 %copy-start.1 = (bf16[64,8,8,128]{3,2,1,0:T(8,128)(2,1)}, bf16[64,8,8,128]{3,2,1,0:T(8,128)(2,1)S(1)}, u32[]{:S(2)}) copy-start(bf16[64,8,8,128]{3,2,1,0:T(8,128)(2,1)S(1)} %copy.54) | copy-start | bytes 3145732
  2.6 3.1 %copy-start.5 = (f32[5,8,512]{2,1,0:T(8,128)S(1)}, f32[5,8,512]{2,1,0:T(8,128)}, u32[]{:S(2)}) copy-start(f32[5,8,512]{2,1,0:T(8,128)} %param.8) | copy-start | bytes 245764
  2.6 3.1 %copy-start.4 = (bf16[512,1024]{1,0:T(8,128)(2,1)S(1)}, bf16[512,1024]{1,0:T(8,128)(2,1)}, u32[]{:S(2)}) copy-start(bf16[512,1024]{1,0:T(8,128)(2,1)} %param.5) | copy-start | bytes 3145732
  4.1 14.0 %collective-permute-start = (f32[8,128,128]{2,1,0:T(8,128)}, f32[8,128,128]{2,1,0:T(8,128)}, u32[]{:S(2)}, u32[]{:S(2)}) collective-permute-start(f32[8,128,128]{2,1,0:T(8,128)} %fusion.17), channel_id=1, source_target_pairs={{0,4},{4,0},{8,12},{12,8},{16,20},{20,16},{24,28},{28,24},{1,5},{5... | collective-permute-start | bytes 1572872 | tf_op jit(solution)/shard_map/ppermute | solution.py:19
  19.2 12.9 %collective-permute-start.1 = (f32[8,128,128]{2,1,0:T(8,128)S(1)}, f32[8,128,128]{2,1,0:T(8,128)S(1)}, u32[]{:S(2)}, u32[]{:S(2)}) collective-permute-start(f32[8,128,128]{2,1,0:T(8,128)S(1)} %fusion.34), channel_id=1, source_target_pairs={{0,8},{8,0},{4,12},{12,4},{16,24},{24,16},{20,28},{28,20},{1,9},{9... | collective-permute-start | bytes 1572872 | tf_op jit(solution)/shard_map/ppermute | solution.py:19
  32.2 14.8 %copy-start.2 = (f32[2,8,256,128]{2,3,1,0:T(8,128)S(1)}, f32[2,8,256,128]{2,3,1,0:T(8,128)}, u32[]{:S(2)}) copy-start(f32[2,8,256,128]{2,3,1,0:T(8,128)} %fusion.5) | copy-start | bytes 6291460
  32.2 14.8 %collective-permute-start.2 = (bf16[8,128,128]{2,1,0:T(8,128)(2,1)S(1)}, bf16[8,128,128]{2,1,0:T(8,128)(2,1)S(1)}, u32[]{:S(2)}, u32[]{:S(2)}) collective-permute-start(bf16[8,128,128]{2,1,0:T(8,128)(2,1)S(1)} %add_convert_fusion), channel_id=1, source_target_pairs={{0,16},{4,20},{8,24},{12,28},{1,17},{5,21},{9,25},{13,29},{2,18},{... | collective-permute-start | bytes 786440 | tf_op jit(solution)/shard_map/ppermute | solution.py:25
  49.3 1.2 %collective-permute-start.3 = (f32[512]{0:T(512)S(1)}, f32[512]{0:T(512)S(1)}, u32[]{:S(2)}, u32[]{:S(2)}) collective-permute-start(f32[512]{0:T(512)S(1)} %bitcast.109), channel_id=1, source_target_pairs={{0,1},{1,0},{2,3},{3,2},{4,5},{5,4},{6,7},{7,6},{8,9},{9,8},{10,11... | collective-permute-start | bytes 6152 | tf_op jit(solution)/shard_map/ppermute | solution.py:100
  50.5 3.6 %collective-permute-start.4 = (f32[512]{0:T(512)S(1)}, f32[512]{0:T(512)S(1)}, u32[]{:S(2)}, u32[]{:S(2)}) collective-permute-start(f32[512]{0:T(512)S(1)} %add.49), channel_id=1, source_target_pairs={{0,2},{1,3},{2,0},{3,1},{4,6},{5,7},{6,4},{7,5},{8,10},{9,11},{10,... | collective-permute-start | bytes 6152 | tf_op jit(solution)/shard_map/ppermute | solution.py:100
  52.0 2.2 %copy-start.6 = (f32[1024]{0:T(1024)S(1)}, f32[1024]{0:T(1024)}, u32[]{:S(2)}) copy-start(f32[1024]{0:T(1024)} %param.9) | copy-start | bytes 12292
